TPU v7x, 128 devices: a whole 4x4x4 slice. The times are simulated.
128 devices in a mesh: space: 32 (over y, x, core), chan: 4 (over z).
Axes of the slice: x: 4, y: 4, z: 4, core: 2. Of those that a mesh axis runs over, the one named last changes fastest.
Arguments:
- features: bfloat16 [128, 16, 256, 128], P('space', None, 'chan'), may hold values from -6 to 6
- fluid_tiles: int32 [32, 4, 8], P('space', None, 'chan'), may hold values from 0 to 1, as said below
- weight_one: bfloat16 [128, 3, 3, 3, 128], replicated, may hold values from -0.109375 to 0.109375
- weight_two: bfloat16 [128, 3, 3, 3, 128], replicated, may hold values from -0.109375 to 0.109375
- weight_three: bfloat16 [128, 3, 3, 3, 128], replicated, may hold values from -0.109375 to 0.109375
- upstream: bfloat16 [64, 8, 128, 128], P('space', None, 'chan'), may hold values from -6 to 6
Outputs:
- coarse_out: bfloat16 [64, 8, 128, 128], P('space', None, 'chan')
- grad_one: float32 [128, 3, 3, 3, 128], P('chan')
- grad_two: float32 [128, 3, 3, 3, 128], P('chan')
- grad_three: float32 [128, 3, 3, 3, 128], P('chan')
Inputs may be any that keep to these rules, and one draw needn't show every extreme that they name: `fluid_tiles`: in each index of the last dimension's 2-tile groups exactly 85 tiles are fluid; all tiles of the first block along the first dimension are fluid.
All inputs are finite; a program needn't handle non-finite values.
Results may differ from a plain program's by a relative error of at most 0.012.
Values may be sent and summed in bfloat16 or wider, within the bound.
A program may use at most 128 MiB of HBM per device.

v0:
```python
import functools

import jax
import jax.numpy as jnp
from jax import lax
from jax.experimental import pallas as pl
from jax.experimental.pallas import tpu as pltpu
from jax.sharding import PartitionSpec as P

TILE_Z = 4
TILE_Y = 32
ROWS = 4
LENGTH = 64
DEPTH = 16
CH = 128
HALF = LENGTH // 2
CELLS = HALF * DEPTH
TAPS = 9 * CH
WIDE = 3 * CH
CHIPS = 4
CHUNKS = 9
BF = jnp.bfloat16
F32 = jnp.float32
MESH = pl.DeviceIdType.MESH


def matmul(left, right):
    return jnp.dot(left, right, preferred_element_type=F32)


def depth_of(shape, axis):
    return lax.broadcasted_iota(jnp.int32, shape, axis) % DEPTH


def combined(wide, step, mirrored):
    first, middle, last = (wide[:, i * CH : (i + 1) * CH] for i in range(3))
    if mirrored:
        first, last = last, first
    rows = wide.shape[0]
    depth = depth_of((rows, CH), 0)
    below = jnp.where(depth >= step, pltpu.roll(first, step, 0), 0.0)
    above = jnp.where(depth < DEPTH - step, pltpu.roll(last, rows - step, 0), 0.0)
    return middle + below + above


def store_transposed(target, slot, values, step):
    depth = depth_of((CH, CH), 1)
    for j in range(values.shape[0] // CH):
        block = jnp.transpose(values[j * CH : (j + 1) * CH, :])
        ahead = jnp.where(depth < DEPTH - step, pltpu.roll(block, CH - step, 1), 0.0)
        behind = jnp.where(depth >= step, pltpu.roll(block, step, 1), 0.0)
        columns = slice(j * CH, (j + 1) * CH)
        target[slot, 0:CH, columns] = ahead.astype(BF)
        target[slot, CH : 2 * CH, columns] = block.astype(BF)
        target[slot, 2 * CH : 3 * CH, columns] = behind.astype(BF)


def gates(values):
    sigma = 0.5 * jnp.tanh(0.5 * values) + 0.5
    return values * sigma, sigma * (1.0 + values * (1.0 - sigma))


def program(
    n_space,
    n_chan,
    feat,
    up,
    mask,
    w1f,
    w2f,
    w3f,
    w2b,
    w3b,
    coarse,
    out1,
    out2,
    out3,
    e1,
    e2,
    e3,
    e4,
    eu,
    d1,
    b2,
    v1f,
    v2f,
    v3f,
    v2b,
    v3b,
    st,
    gt,
    cf,
    part,
    cs,
    cr,
    zs,
    zr,
    xs,
    xr,
    ys,
    yr,
    fs,
    fr,
    send_sem,
    recv_sem,
    local_sem,
):
    space = lax.axis_index("space")
    chan = lax.axis_index("chan")
    core = lax.rem(space, 2)
    chip_x = lax.rem(lax.div(space, 2), CHIPS)
    chip_y = lax.div(space, 2 * CHIPS)

    def near(d_space, d_chan):
        return (
            lax.rem(space + (d_space + n_space), n_space),
            lax.rem(chan + (d_chan + n_chan), n_chan),
        )

    sibling = (space + 1 - 2 * core, chan)

    def x_peer(d):
        return (chip_y * (2 * CHIPS) + lax.rem(chip_x + d, CHIPS) * 2 + core, chan)

    def y_peer(d):
        return (lax.rem(chip_y + d, CHIPS) * (2 * CHIPS) + chip_x * 2 + core, chan)

    started = []

    def send(source, target, device):
        index = len(started)
        copy = pltpu.make_async_remote_copy(
            src_ref=source,
            dst_ref=target,
            send_sem=send_sem.at[index],
            recv_sem=recv_sem.at[index],
            device_id=device,
            device_id_type=MESH,
        )
        copy.start()
        started.append(copy)
        return copy

    local = []

    def fetch(source, target):
        copy = pltpu.make_async_copy(source, target, local_sem.at[len(local)])
        copy.start()
        local.append(copy)
        return copy

    peers = [near(a, b) for a in (-1, 0, 1) for b in (-1, 0, 1) if (a, b) != (0, 0)]
    peers.append(near(0, 2))
    peers += [x_peer(d) for d in range(1, CHIPS)]
    peers += [y_peer(d) for d in range(1, CHIPS)]
    barrier = pltpu.get_barrier_semaphore()
    for peer in peers:
        pl.semaphore_signal(barrier, inc=1, device_id=peer, device_id_type=MESH)
    get_e1 = fetch(feat, e1.at[pl.ds(1, ROWS), pl.ds(1, LENGTH)])
    get_eu = fetch(up, eu.at[pl.ds(0, 2), pl.ds(0, HALF)])
    get_v1f = fetch(w1f, v1f)
    get_v3b = fetch(w3b, v3b)
    get_v2f = fetch(w2f, v2f)
    get_v3f = fetch(w3f, v3f)
    get_v2b = fetch(w2b, v2b)
    pl.semaphore_wait(barrier, len(peers))

    in_x, in_y = pl.ds(1, ROWS), pl.ds(1, LENGTH)
    halo_one = [
        send(feat.at[ROWS - 1], e1.at[0, in_y], near(1, 0)),
        send(feat.at[0], e1.at[ROWS + 1, in_y], near(-1, 0)),
        send(feat.at[:, LENGTH - 1], e1.at[in_x, 0], near(0, 1)),
        send(feat.at[:, 0], e1.at[in_x, LENGTH + 1], near(0, -1)),
        send(feat.at[ROWS - 1, LENGTH - 1], e1.at[0, 0], near(1, 1)),
        send(feat.at[ROWS - 1, 0], e1.at[0, LENGTH + 1], near(1, -1)),
        send(feat.at[0, LENGTH - 1], e1.at[ROWS + 1, 0], near(-1, 1)),
        send(feat.at[0, 0], e1.at[ROWS + 1, LENGTH + 1], near(-1, -1)),
    ]
    halo_up = [
        send(up.at[0], eu.at[2, pl.ds(0, HALF)], near(-1, 0)),
        send(up.at[:, 0], eu.at[pl.ds(0, 2), HALF], near(0, -1)),
        send(up.at[0, 0], eu.at[2, HALF], near(-1, -1)),
    ]

    def arrived(copies):
        for copy in copies:
            copy.wait_recv()

    def clear(ref, width):
        rows, columns = ref.shape[0], ref.shape[1]

        @pl.when(space == 0)
        def _():
            ref[0:width] = jnp.zeros((width, columns, DEPTH, CH), BF)

        @pl.when(space == n_space - 1)
        def _():
            ref[rows - width : rows] = jnp.zeros((width, columns, DEPTH, CH), BF)

        @pl.when(chan == 0)
        def _():
            ref[:, 0:width] = jnp.zeros((rows, width, DEPTH, CH), BF)

        @pl.when(chan == n_chan - 1)
        def _():
            ref[:, columns - width : columns] = jnp.zeros((rows, width, DEPTH, CH), BF)

    def rim(ref, low):
        y = pl.ds(2, LENGTH)
        if low:
            near_rows, far_rows, to = pl.ds(2, 2), pl.ds(ROWS + 2, 2), -1
        else:
            near_rows, far_rows, to = pl.ds(ROWS, 2), pl.ds(0, 2), 1
        first, last = pl.ds(2, 2), pl.ds(LENGTH, 2)
        before, after = pl.ds(0, 2), pl.ds(LENGTH + 2, 2)
        return [
            send(ref.at[near_rows, y], ref.at[far_rows, y], near(to, 0)),
            send(ref.at[near_rows, last], ref.at[far_rows, before], near(to, 1)),
            send(ref.at[near_rows, first], ref.at[far_rows, after], near(to, -1)),
        ]

    def sides(ref):
        x = pl.ds(2, ROWS)
        return [
            send(ref.at[x, pl.ds(LENGTH, 2)], ref.at[x, pl.ds(0, 2)], near(0, 1)),
            send(ref.at[x, pl.ds(2, 2)], ref.at[x, pl.ds(LENGTH + 2, 2)], near(0, -1)),
        ]

    def flat(block):
        return block.reshape(-1, CH)

    def window(ref, x, begin, spread):
        return jnp.concatenate(
            [
                flat(ref[x + spread * ax, pl.ds(begin + spread * ay, HALF)])
                for ax in range(3)
                for ay in range(3)
            ],
            axis=1,
        )

    def fluid(half):
        cells = jnp.broadcast_to(mask[half][None], (HALF, DEPTH, CH))
        return flat(cells)

    def over(low, high, step):
        def one(i, carry):
            step(lax.div(i, 2), lax.rem(i, 2))
            return carry

        lax.fori_loop(low, high, one, 0)

    get_eu.wait()
    for qx in range(2):
        store_transposed(gt, qx, flat(eu[qx, 0:HALF]).astype(F32), 1)

    get_e1.wait()
    get_v1f.wait()
    arrived(halo_one)
    clear(e1, 1)

    def layer_one(x, half):
        pre = combined(matmul(window(e1, x, half * HALF, 1), v1f[...]), 1, False)
        hidden, slope = gates(pre)
        inside = fluid(half)
        block = (hidden * inside).astype(BF).reshape(HALF, DEPTH, CH)
        e2[2 + x, pl.ds(2 + half * HALF, HALF)] = block
        d1[x, half] = slope * inside

    over(0, 4, layer_one)
    halo_two = rim(e2, True)
    over(4, 8, layer_one)
    halo_two += rim(e2, False)
    halo_two += sides(e2)

    arrived(halo_up)
    get_v3b.wait()

    @pl.when(space == n_space - 1)
    def _():
        eu[2] = jnp.zeros((HALF + 1, DEPTH, CH), BF)

    @pl.when(chan == n_chan - 1)
    def _():
        eu[:, HALF] = jnp.zeros((3, DEPTH, CH), BF)

    routes = (((1, 0),), ((0, 1), (2, 0)))
    for qx in range(2):
        for px in range(2):
            for py in range(2):
                taps = [(ax, dx, ay, dy) for ax, dx in routes[px] for ay, dy in routes[py]]
                cells = [flat(eu[qx + dx, dy : dy + HALF]) for _, dx, _, dy in taps]
                rows = [v3b[(ax * 3 + ay) * CH : (ax * 3 + ay + 1) * CH, :] for ax, _, ay, _ in taps]
                if len(taps) > 1:
                    cells, rows = [jnp.concatenate(cells, axis=1)], [jnp.concatenate(rows, axis=0)]
                back = combined(matmul(cells[0], rows[0]), 1, True)
                b2[2 * qx + px, py] = back.astype(BF).reshape(HALF, DEPTH, CH)

    get_v2f.wait()
    arrived(halo_two)
    clear(e2, 2)

    def layer_two(x, half):
        pre = combined(matmul(window(e2, x, half * HALF, 2), v2f[...]), 2, False)
        hidden, slope = gates(pre)
        inside = fluid(half)
        pairs = (hidden * inside).astype(BF).reshape(HALF // 2, 2, DEPTH, CH)
        first = half * (HALF // 2)
        e3[1 + x, 1, pl.ds(first, HALF // 2)] = pairs[:, 0]
        e3[1 + x, 0, pl.ds(first + 1, HALF // 2)] = pairs[:, 1]
        back = [b2[x, r, pl.ds(first, HALF // 2)].astype(F32) for r in range(2)]
        back = flat(jnp.stack(back, axis=1))
        product = (back * inside * slope).astype(BF)
        e4[2 + x, pl.ds(2 + half * HALF, HALF)] = product.reshape(HALF, DEPTH, CH)
        store_transposed(st, 2 * x + half, product.astype(F32), 2)

    over(0, 4, layer_two)
    halo_four = rim(e4, True)
    over(4, 8, layer_two)
    halo_four += rim(e4, False)
    halo_four += sides(e4)
    evens, odds = pl.ds(0, HALF), pl.ds(1, HALF)
    halo_three = [
        send(e3.at[ROWS, 1, evens], e3.at[0, 1, evens], near(1, 0)),
        send(e3.at[ROWS, 0, odds], e3.at[0, 0, odds], near(1, 0)),
        send(e3.at[pl.ds(1, ROWS), 0, HALF], e3.at[pl.ds(1, ROWS), 0, 0], near(0, 1)),
        send(e3.at[ROWS, 0, HALF], e3.at[0, 0, 0], near(1, 1)),
    ]

    waits = {}

    def share_core(k):
        cs[k] = part[k, :, :, 1 - core].astype(BF)
        waits[k] = [send(cs.at[k], cr.at[k], sibling)]

    def share_chan(k):
        arrived(waits[k])
        waits[k] = []
        for d in range(1, n_chan):
            other = lax.rem(chan + d, n_chan)
            zs[k, d - 1] = (part[k, :, other, core] + cr[k, :, other].astype(F32)).astype(BF)
            waits[k].append(send(zs.at[k, d - 1], zr.at[k, d - 1], near(0, d)))

    def share_first(k):
        arrived(waits[k])
        total = part[k, :, chan, core] + cr[k, :, chan].astype(F32)
        for d in range(1, n_chan):
            total += zr[k, d - 1].astype(F32)
        xs[k] = total.astype(BF)
        peer = (x_peer, y_peer)[k % 2]
        waits[k] = [send(xs.at[k], xr.at[k, d - 1], peer(d)) for d in range(1, CHIPS)]

    def four(own, others, k):
        opposite = own[k].astype(F32) + others[k, 1].astype(F32)
        return opposite + (others[k, 0].astype(F32) + others[k, 2].astype(F32))

    def share_second(k):
        arrived(waits[k])
        ys[k] = four(xs, xr, k).astype(BF)
        peer = (y_peer, x_peer)[k % 2]
        waits[k] = [send(ys.at[k], yr.at[k, d - 1], peer(d)) for d in range(1, CHIPS)]

    def share_back(k):
        arrived(waits[k])
        total = four(ys, yr, k)
        fs[k] = jnp.concatenate([total[0], total[1], total[2]], axis=1)
        waits[k] = [send(fs.at[k], fr.at[k], sibling)]

    def finish(k):
        arrived(waits[k])
        out = (out2, out3, out1)[k // 3]
        columns = slice((k % 3) * TAPS, (k % 3 + 1) * TAPS)
        out[core, :, columns] = fs[k]
        out[1 - core, :, columns] = fr[k]

    stages = (share_core, share_chan, share_first, share_second, share_back, finish)
    progress = {}

    def advance(*chunks):
        for k in chunks:
            at = progress.get(k, 0)
            if at < len(stages):
                stages[at](k)
                progress[k] = at + 1

    def grads(k, ref, spread):
        ax = k % 3
        part[k] = jnp.zeros(part.shape[1:], F32)

        def one(x, carry):
            slopes = jnp.concatenate([st[2 * x], st[2 * x + 1]], axis=1)
            cells = [
                flat(ref[x + spread * ax, spread * ay : spread * ay + LENGTH]) for ay in range(3)
            ]
            product = matmul(slopes, jnp.concatenate(cells, axis=1))
            part[k] += product.reshape(part.shape[1:])
            return carry

        lax.fori_loop(0, ROWS, one, 0)

    def coarse_window(x):
        return [flat(e3[x, r, j : j + HALF]) for r, j in ((0, 0), (1, 0), (0, 1))]

    def coarse_grads(k):
        ax = k % 3
        total = 0.0
        for qx in range(2):
            cells = jnp.concatenate(coarse_window(2 * qx + ax), axis=1)
            total += matmul(gt[qx], cells)
        part[k] = total.reshape(part.shape[1:])

    for k in range(3):
        grads(k, e2, 2)
        advance(*range(k + 1))
    arrived(halo_three)
    get_v3f.wait()

    @pl.when(space == 0)
    def _():
        e3[0] = jnp.zeros(e3.shape[1:], BF)

    @pl.when(chan == 0)
    def _():
        e3[:, 0, 0] = jnp.zeros((ROWS + 1, DEPTH, CH), BF)

    for k in range(3, 6):
        coarse_grads(k)
        advance(*range(k + 1))
    for qx in range(2):
        cells = [block for ax in range(3) for block in coarse_window(2 * qx + ax)]
        cf[...] = combined(matmul(jnp.concatenate(cells, axis=1), v3f[...]), 1, False)
        for qz in range(DEPTH // 2):
            coarse[qx, qz] = cf[pl.ds(2 * qz, HALF, stride=DEPTH), :].astype(BF)
    advance(*range(6))
    get_v2b.wait()
    arrived(halo_four)
    clear(e4, 2)

    def layer_back(x, half):
        back = combined(matmul(mirror(x, half), v2b[...]), 2, True).astype(BF).astype(F32)
        slope = (back * d1[x, half]).astype(BF)
        store_transposed(st, 2 * x + half, slope.astype(F32), 1)

    def mirror(x, half):
        return jnp.concatenate(
            [
                flat(e4[x + 4 - 2 * ax, pl.ds(half * HALF + 4 - 2 * ay, HALF)])
                for ax in range(3)
                for ay in range(3)
            ],
            axis=1,
        )

    over(0, 4, layer_back)
    advance(*range(6))
    over(4, 8, layer_back)
    advance(*range(6))
    for k in range(6, 9):
        grads(k, e1, 1)
        advance(*range(k + 1))
    while any(progress[k] < len(stages) for k in range(CHUNKS)):
        advance(*range(CHUNKS))
    for copy in started:
        copy.wait_send()


def local(features, fluid_tiles, weight_one, weight_two, weight_three, upstream, sizes):
    n_space, n_chan = sizes
    feat = jnp.transpose(features, (0, 2, 1, 3))
    up = jnp.transpose(upstream, (0, 2, 1, 3))
    up = jnp.stack([up, jnp.zeros_like(up)], axis=3).reshape(2, HALF, DEPTH, CH)
    tiles = jnp.transpose(fluid_tiles[0], (1, 0)).astype(F32)
    mask = jnp.broadcast_to(jnp.repeat(tiles, TILE_Z, axis=1)[:, :, None], (2, DEPTH, CH))

    def forward(weight):
        return jnp.transpose(weight, (1, 3, 4, 2, 0)).reshape(TAPS, WIDE)

    def backward(weight):
        return jnp.transpose(weight, (1, 3, 0, 2, 4)).reshape(TAPS, WIDE)

    hbm = pl.BlockSpec(memory_space=pl.ANY)
    vmem = pl.BlockSpec(memory_space=pltpu.VMEM)
    grad_shape = jax.ShapeDtypeStruct((2, 16, 3 * TAPS), F32)
    copies = 31 + 11 * CHUNKS
    weight_shape = pltpu.VMEM((TAPS, WIDE), BF)
    piece = (CHUNKS, 3, 16, WIDE)
    pieces = (CHUNKS, 3, 3, 16, WIDE)
    coarse, grad_one, grad_two, grad_three = pl.pallas_call(
        functools.partial(program, n_space, n_chan),
        out_shape=(
            jax.ShapeDtypeStruct((2, DEPTH // 2, HALF, CH), BF),
            grad_shape,
            grad_shape,
            grad_shape,
        ),
        in_specs=[hbm, hbm, vmem, hbm, hbm, hbm, hbm, hbm],
        out_specs=[vmem] * 4,
        scratch_shapes=[
            pltpu.VMEM((ROWS + 2, LENGTH + 2, DEPTH, CH), BF),
            pltpu.VMEM((ROWS + 4, LENGTH + 4, DEPTH, CH), BF),
            pltpu.VMEM((ROWS + 1, 2, HALF + 1, DEPTH, CH), BF),
            pltpu.VMEM((ROWS + 4, LENGTH + 4, DEPTH, CH), BF),
            pltpu.VMEM((3, HALF + 1, DEPTH, CH), BF),
            pltpu.VMEM((ROWS, 2, CELLS, CH), F32),
            pltpu.VMEM((ROWS, 2, HALF, DEPTH, CH), BF),
            weight_shape,
            weight_shape,
            weight_shape,
            weight_shape,
            weight_shape,
            pltpu.VMEM((8, WIDE, CELLS), BF),
            pltpu.VMEM((2, WIDE, CELLS), BF),
            pltpu.VMEM((CELLS, CH), F32),
            pltpu.VMEM((CHUNKS, 3, n_chan, 2, 16, WIDE), F32),
            pltpu.VMEM((CHUNKS, 3, n_chan, 16, WIDE), BF),
            pltpu.VMEM((CHUNKS, 3, n_chan, 16, WIDE), BF),
            pltpu.VMEM(pieces, BF),
            pltpu.VMEM(pieces, BF),
            pltpu.VMEM(piece, BF),
            pltpu.VMEM(pieces, BF),
            pltpu.VMEM(piece, BF),
            pltpu.VMEM(pieces, BF),
            pltpu.VMEM((CHUNKS, 16, TAPS), F32),
            pltpu.VMEM((CHUNKS, 16, TAPS), F32),
            pltpu.SemaphoreType.DMA((copies,)),
            pltpu.SemaphoreType.DMA((copies,)),
            pltpu.SemaphoreType.DMA((7,)),
        ],
        compiler_params=pltpu.CompilerParams(
            collective_id=0, has_side_effects=True, vmem_limit_bytes=58 << 20
        ),
    )(
        feat,
        up,
        mask,
        forward(weight_one),
        forward(weight_two),
        forward(weight_three),
        backward(weight_two),
        backward(weight_three),
    )
    shape = (2 * 16, 3, 3, 3, CH)
    return (
        coarse,
        grad_one.reshape(shape),
        grad_two.reshape(shape),
        grad_three.reshape(shape),
    )


def solution(mesh):
    in_specs = (
        P("space", None, "chan", None),
        P("space", None, "chan"),
        P(),
        P(),
        P(),
        P("space", None, "chan", None),
    )
    out_specs = (
        P("space", None, "chan", None),
        P("chan", None, None, None, None),
        P("chan", None, None, None, None),
        P("chan", None, None, None, None),
    )
    sizes = (mesh.shape["space"], mesh.shape["chan"])
    return jax.shard_map(
        functools.partial(local, sizes=sizes),
        mesh=mesh,
        in_specs=in_specs,
        out_specs=out_specs,
        check_vma=False,
    )
```

profile of v0, /device:TPU:1, one launch (start us, length us, event | category | flops | bytes accessed | tf_op | source)
XLA Modules:
  0.0 135.1 jit_solution(7057072295877243419)
XLA Ops:
  0.6 2.0 %copy.25 = bf16[3,3,128,3,128]{4,3,2,1,0:T(4,128)(2,1)S(1)} copy(bf16[3,3,128,3,128]{4,2,1,3,0:T(8,128)(2,1)} %bitcast.43) | data formatting | bytes 1769472 | tf_op jit(solution)/shard_map/transpose | solution.py:479
  2.7 0.8 copy.26
  3.4 1.6 %copy_bitcast_fusion.1 = (bf16[1152,384]{1,0:T(8,128)(2,1)}, bf16[1152,384]{1,0:T(8,128)(2,1)}) fusion(bf16[144,8,3,128]{3,2,1,0:T(4,128)(2,1)S(1)} %bitcast.39, bf16[144,8,3,128]{3,2,1,0:T(4,128)(2,1)S(1)} %bitcast.38), kind=kLoop, calls=%fused_computation.1 | loop fusion | bytes 3538944 | tf_op jit(solution)/shard_map/reshape | solution.py:479
  5.1 0.8 copy.23
  5.9 0.8 copy.24
  6.8 1.5 %copy_bitcast_fusion.3 = (bf16[1152,384]{1,0:T(8,128)(2,1)}, bf16[1152,384]{1,0:T(8,128)(2,1)}) fusion(bf16[144,8,3,128]{3,2,1,0:T(4,128)(2,1)S(1)} %bitcast.41, bf16[144,8,3,128]{3,2,1,0:T(4,128)(2,1)S(1)} %bitcast.40), kind=kLoop, calls=%fused_computation.3 | loop fusion | bytes 3538944 | tf_op jit(solution)/shard_map/reshape | solution.py:476
  8.3 0.8 copy.22
  9.2 1.1 copy.43
  10.3 0.4 copy-done.2
  10.7 1.6 %copy.42 = bf16[4,16,64,128]{3,1,2,0:T(8,128)(2,1)} copy(bf16[4,16,64,128]{3,2,1,0:T(8,128)(2,1)S(1)} %copy-done.2) | data formatting | bytes 2097152 | tf_op args[0]
  12.4 0.2 copy.30
  12.6 1.0 stack.7.clone
  13.5 0.1 broadcast_in_dim.10
  13.6 0.1 broadcast_in_dim.11
  13.7 0.7 broadcast_in_dim.12.mask
  14.4 116.0 %shard_map.93 = (bf16[2,8,32,128]{3,2,1,0:T(8,128)(2,1)}, f32[2,16,3456]{2,1,0:T(8,128)}, f32[2,16,3456]{2,1,0:T(8,128)}, f32[2,16,3456]{2,1,0:T(8,128)}) custom-call(bf16[4,64,16,128]{3,2,1,0:T(8,128)(2,1)} %bitcast.42, bf16[2,32,16,128]{3,2,1,0:T(8,128)(2,1)} %bitcast.48, f32[2,16,128]{2,1,0:T(8,128)} %broadcast_in_dim.12.mask, ...), custom_call_target="tpu_custom_call" | custom-call | tf_op jit(solution)/shard_map/pallas_call | solution.py:488
  130.4 1.2 reshape.43
  131.6 0.8 copy.27
  132.4 0.2 reshape.44
  132.6 0.8 copy.28
  133.4 0.0 copy-done.4
  133.4 0.2 reshape.45
  133.6 0.8 copy.29
  134.4 0.7 copy.45
  (17 shorter events, 0.0 us)
Async XLA Ops:
  0.6 2.0 %copy-start.1 = (bf16[128,3,3,3,128]{4,0,3,2,1:T(8,128)(2,1)S(1)}, bf16[128,3,3,3,128]{4,0,3,2,1:T(8,128)(2,1)}, u32[]{:S(2)}) copy-start(bf16[128,3,3,3,128]{4,0,3,2,1:T(8,128)(2,1)} %param.10) | copy-start | bytes 2654212
  3.4 1.6 %copy-start = (bf16[128,3,3,3,128]{4,0,3,2,1:T(8,128)(2,1)S(1)}, bf16[128,3,3,3,128]{4,0,3,2,1:T(8,128)(2,1)}, u32[]{:S(2)}) copy-start(bf16[128,3,3,3,128]{4,0,3,2,1:T(8,128)(2,1)} %param.9) | copy-start | bytes 2654212
  6.8 1.5 %copy-start.3 = (bf16[128,3,3,3,128]{4,0,3,2,1:T(8,128)(2,1)S(1)}, bf16[128,3,3,3,128]{4,0,3,2,1:T(8,128)(2,1)}, u32[]{:S(2)}) copy-start(bf16[128,3,3,3,128]{4,0,3,2,1:T(8,128)(2,1)} %param.8) | copy-start | bytes 2654212
  9.2 1.5 %copy-start.2 = (bf16[4,16,64,128]{3,2,1,0:T(8,128)(2,1)S(1)}, bf16[4,16,64,128]{3,2,1,0:T(8,128)(2,1)}, u32[]{:S(2)}) copy-start(bf16[4,16,64,128]{3,2,1,0:T(8,128)(2,1)} %param.6) | copy-start | bytes 3145732
  10.3 2.1 %copy-start.6 = (bf16[2,8,32,128]{3,2,1,0:T(8,128)(2,1)S(1)}, bf16[2,8,32,128]{3,2,1,0:T(8,128)(2,1)}, u32[]{:S(2)}) copy-start(bf16[2,8,32,128]{3,2,1,0:T(8,128)(2,1)} %param.11) | copy-start | bytes 393220
  10.7 2.8 %copy-start.8 = (s32[1,4,2]{1,2,0:T(2,128)S(1)}, s32[1,4,2]{1,2,0:T(2,128)}, u32[]{:S(2)}) copy-start(s32[1,4,2]{1,2,0:T(2,128)} %param.7) | copy-start | bytes 100
  130.4 2.1 %copy-start.5 = (f32[2,16,3456]{2,1,0:T(8,128)S(1)}, f32[2,16,3456]{2,1,0:T(8,128)}, u32[]{:S(2)}) copy-start(f32[2,16,3456]{2,1,0:T(8,128)} %get-tuple-element.10) | copy-start | bytes 1327108
  132.4 1.0 copy-start.4
  133.4 1.0 copy-start.7
where the time goes:
time: 135 us
  Pallas kernels  116 us (86%)
  local copies, waits for them, and re-layouts  18.4 us (14%)
    pallas_call x1, Pallas kernels, local(): pl.pallas_call(functools.partial(program, n_space, n_chan), out_shape=(ja...  116 us
    unnamed x25, local copies, waits for them, and re-layouts  6.54 us
    transpose x2, local copies, waits for them, and re-layouts, backward(): return jnp.transpose(weight, (1, 3, 0, 2, 4)).reshape(TAPS, WIDE)  2.78 us

commit v1 on v0

--- a/solution.py
+++ b/solution.py
@@ -24,23 +24,33 @@
 MESH = pl.DeviceIdType.MESH
 
 
+def matmul_transposed(left, right):
+    return lax.dot_general(left, right, (((1,), (1,)), ((), ())), preferred_element_type=F32)
+
+
 def matmul(left, right):
     return jnp.dot(left, right, preferred_element_type=F32)
 
 
 def depth_of(shape, axis):
-    return lax.broadcasted_iota(jnp.int32, shape, axis) % DEPTH
+    return lax.broadcasted_iota(jnp.int32, shape, axis) & (DEPTH - 1)
+
+
+def rotated(values, step):
+    turned = pltpu.roll(values.reshape(-1, 8, CH), step, 1)
+    return turned.reshape(-1, 2, 8, CH)
 
 
 def combined(wide, step, mirrored):
     first, middle, last = (wide[:, i * CH : (i + 1) * CH] for i in range(3))
     if mirrored:
         first, last = last, first
-    rows = wide.shape[0]
-    depth = depth_of((rows, CH), 0)
-    below = jnp.where(depth >= step, pltpu.roll(first, step, 0), 0.0)
-    above = jnp.where(depth < DEPTH - step, pltpu.roll(last, rows - step, 0), 0.0)
-    return middle + below + above
+    depth = lax.broadcasted_iota(jnp.int32, (1, 8, CH), 1)
+    low, high = depth < step, depth >= 8 - step
+    down, up = rotated(first, step), rotated(last, 8 - step)
+    upper = jnp.where(low, 0.0, down[:, 0]) + jnp.where(high, up[:, 1], up[:, 0])
+    lower = jnp.where(low, down[:, 0], down[:, 1]) + jnp.where(high, 0.0, up[:, 1])
+    return middle + jnp.stack([upper, lower], axis=1).reshape(-1, CH)
 
 
 def store_transposed(target, slot, values, step):
@@ -65,12 +75,10 @@
     n_chan,
     feat,
     up,
-    mask,
-    w1f,
-    w2f,
-    w3f,
-    w2b,
-    w3b,
+    tiles,
+    w1,
+    w2,
+    w3,
     coarse,
     out1,
     out2,
@@ -90,6 +98,9 @@
     st,
     gt,
     cf,
+    raw_x,
+    raw_up,
+    wide,
     part,
     cs,
     cr,
@@ -156,30 +167,61 @@
     barrier = pltpu.get_barrier_semaphore()
     for peer in peers:
         pl.semaphore_signal(barrier, inc=1, device_id=peer, device_id_type=MESH)
-    get_e1 = fetch(feat, e1.at[pl.ds(1, ROWS), pl.ds(1, LENGTH)])
-    get_eu = fetch(up, eu.at[pl.ds(0, 2), pl.ds(0, HALF)])
-    get_v1f = fetch(w1f, v1f)
-    get_v3b = fetch(w3b, v3b)
-    get_v2f = fetch(w2f, v2f)
-    get_v3f = fetch(w3f, v3f)
-    get_v2b = fetch(w2b, v2b)
+    get_x = fetch(feat, raw_x)
+    get_up = fetch(up, raw_up)
+
+    def forward_weight(source, target):
+        return [fetch(source.at[:, az], target.at[:, :, az]) for az in range(3)]
+
+    def backward_weight(source, target):
+        return [
+            fetch(source.at[:, az], target.at[:, :, :, az * CH : (az + 1) * CH])
+            for az in range(3)
+        ]
+
+    get_v1f = forward_weight(w1, v1f)
+    get_v3b = backward_weight(w3, v3b)
+    get_v2f = forward_weight(w2, v2f)
+    get_v3f = forward_weight(w3, v3f)
+    get_v2b = backward_weight(w2, v2b)
+
+    def ready(copies):
+        for copy in copies:
+            copy.wait()
+
+    get_x.wait()
+
+    def turn(x, carry):
+        for z in range(DEPTH):
+            wide[pl.ds(z, LENGTH, stride=DEPTH), :] = raw_x[x, z].astype(F32)
+        e1[1 + x, pl.ds(1, LENGTH)] = wide[...].astype(BF).reshape(LENGTH, DEPTH, CH)
+        return carry
+
+    lax.fori_loop(0, ROWS, turn, 0)
+    get_up.wait()
+    cf[...] = jnp.zeros_like(cf)
+    for qx in range(2):
+        for qz in range(DEPTH // 2):
+            cf[pl.ds(2 * qz, HALF, stride=DEPTH), :] = raw_up[qx, qz].astype(F32)
+        eu[qx, 0:HALF] = cf[...].astype(BF).reshape(HALF, DEPTH, CH)
     pl.semaphore_wait(barrier, len(peers))
 
     in_x, in_y = pl.ds(1, ROWS), pl.ds(1, LENGTH)
+    top, right = ROWS, LENGTH
     halo_one = [
-        send(feat.at[ROWS - 1], e1.at[0, in_y], near(1, 0)),
-        send(feat.at[0], e1.at[ROWS + 1, in_y], near(-1, 0)),
-        send(feat.at[:, LENGTH - 1], e1.at[in_x, 0], near(0, 1)),
-        send(feat.at[:, 0], e1.at[in_x, LENGTH + 1], near(0, -1)),
-        send(feat.at[ROWS - 1, LENGTH - 1], e1.at[0, 0], near(1, 1)),
-        send(feat.at[ROWS - 1, 0], e1.at[0, LENGTH + 1], near(1, -1)),
-        send(feat.at[0, LENGTH - 1], e1.at[ROWS + 1, 0], near(-1, 1)),
-        send(feat.at[0, 0], e1.at[ROWS + 1, LENGTH + 1], near(-1, -1)),
+        send(e1.at[top, in_y], e1.at[0, in_y], near(1, 0)),
+        send(e1.at[1, in_y], e1.at[top + 1, in_y], near(-1, 0)),
+        send(e1.at[in_x, right], e1.at[in_x, 0], near(0, 1)),
+        send(e1.at[in_x, 1], e1.at[in_x, right + 1], near(0, -1)),
+        send(e1.at[top, right], e1.at[0, 0], near(1, 1)),
+        send(e1.at[top, 1], e1.at[0, right + 1], near(1, -1)),
+        send(e1.at[1, right], e1.at[top + 1, 0], near(-1, 1)),
+        send(e1.at[1, 1], e1.at[top + 1, right + 1], near(-1, -1)),
     ]
     halo_up = [
-        send(up.at[0], eu.at[2, pl.ds(0, HALF)], near(-1, 0)),
-        send(up.at[:, 0], eu.at[pl.ds(0, 2), HALF], near(0, -1)),
-        send(up.at[0, 0], eu.at[2, HALF], near(-1, -1)),
+        send(eu.at[0, pl.ds(0, HALF)], eu.at[2, pl.ds(0, HALF)], near(-1, 0)),
+        send(eu.at[pl.ds(0, 2), 0], eu.at[pl.ds(0, 2), HALF], near(0, -1)),
+        send(eu.at[0, 0], eu.at[2, HALF], near(-1, -1)),
     ]
 
     def arrived(copies):
@@ -240,8 +282,16 @@
         )
 
     def fluid(half):
-        cells = jnp.broadcast_to(mask[half][None], (HALF, DEPTH, CH))
+        depth = lax.broadcasted_iota(jnp.int32, (DEPTH, CH), 0)
+        column = jnp.zeros((DEPTH, CH), jnp.int32)
+        for i in range(DEPTH // TILE_Z):
+            column = jnp.where(lax.div(depth, TILE_Z) == i, tiles[0, half, i], column)
+        cells = jnp.broadcast_to(column.astype(F32)[None], (HALF, DEPTH, CH))
         return flat(cells)
+
+    def taps_of(weight):
+        blocks = [weight[ax, ay].reshape(WIDE, CH) for ax in range(3) for ay in range(3)]
+        return jnp.concatenate(blocks, axis=1)
 
     def over(low, high, step):
         def one(i, carry):
@@ -250,17 +300,15 @@
 
         lax.fori_loop(low, high, one, 0)
 
-    get_eu.wait()
     for qx in range(2):
         store_transposed(gt, qx, flat(eu[qx, 0:HALF]).astype(F32), 1)
 
-    get_e1.wait()
-    get_v1f.wait()
+    ready(get_v1f)
     arrived(halo_one)
     clear(e1, 1)
 
     def layer_one(x, half):
-        pre = combined(matmul(window(e1, x, half * HALF, 1), v1f[...]), 1, False)
+        pre = combined(matmul_transposed(window(e1, x, half * HALF, 1), taps_of(v1f)), 1, False)
         hidden, slope = gates(pre)
         inside = fluid(half)
         block = (hidden * inside).astype(BF).reshape(HALF, DEPTH, CH)
@@ -274,7 +322,7 @@
     halo_two += sides(e2)
 
     arrived(halo_up)
-    get_v3b.wait()
+    ready(get_v3b)
 
     @pl.when(space == n_space - 1)
     def _():
@@ -290,18 +338,18 @@
             for py in range(2):
                 taps = [(ax, dx, ay, dy) for ax, dx in routes[px] for ay, dy in routes[py]]
                 cells = [flat(eu[qx + dx, dy : dy + HALF]) for _, dx, _, dy in taps]
-                rows = [v3b[(ax * 3 + ay) * CH : (ax * 3 + ay + 1) * CH, :] for ax, _, ay, _ in taps]
+                rows = [v3b[ax, ay] for ax, _, ay, _ in taps]
                 if len(taps) > 1:
                     cells, rows = [jnp.concatenate(cells, axis=1)], [jnp.concatenate(rows, axis=0)]
                 back = combined(matmul(cells[0], rows[0]), 1, True)
                 b2[2 * qx + px, py] = back.astype(BF).reshape(HALF, DEPTH, CH)
 
-    get_v2f.wait()
+    ready(get_v2f)
     arrived(halo_two)
     clear(e2, 2)
 
     def layer_two(x, half):
-        pre = combined(matmul(window(e2, x, half * HALF, 2), v2f[...]), 2, False)
+        pre = combined(matmul_transposed(window(e2, x, half * HALF, 2), taps_of(v2f)), 2, False)
         hidden, slope = gates(pre)
         inside = fluid(half)
         pairs = (hidden * inside).astype(BF).reshape(HALF // 2, 2, DEPTH, CH)
@@ -363,15 +411,16 @@
     def share_back(k):
         arrived(waits[k])
         total = four(ys, yr, k)
-        fs[k] = jnp.concatenate([total[0], total[1], total[2]], axis=1)
+        fs[k] = total
         waits[k] = [send(fs.at[k], fr.at[k], sibling)]
 
     def finish(k):
         arrived(waits[k])
         out = (out2, out3, out1)[k // 3]
-        columns = slice((k % 3) * TAPS, (k % 3 + 1) * TAPS)
-        out[core, :, columns] = fs[k]
-        out[1 - core, :, columns] = fr[k]
+        for ay in range(3):
+            columns = slice(ay * CH, (ay + 1) * CH)
+            out[k % 3, :, ay, core] = fs[k, :, :, columns]
+            out[k % 3, :, ay, 1 - core] = fr[k, :, :, columns]
 
     stages = (share_core, share_chan, share_first, share_second, share_back, finish)
     progress = {}
@@ -385,18 +434,21 @@
 
     def grads(k, ref, spread):
         ax = k % 3
-        part[k] = jnp.zeros(part.shape[1:], F32)
-
-        def one(x, carry):
-            slopes = jnp.concatenate([st[2 * x], st[2 * x + 1]], axis=1)
-            cells = [
-                flat(ref[x + spread * ax, spread * ay : spread * ay + LENGTH]) for ay in range(3)
-            ]
-            product = matmul(slopes, jnp.concatenate(cells, axis=1))
-            part[k] += product.reshape(part.shape[1:])
-            return carry
-
-        lax.fori_loop(0, ROWS, one, 0)
+        slopes = jnp.concatenate([st[i] for i in range(2 * ROWS)], axis=1)
+        cells = jnp.concatenate(
+            [
+                jnp.concatenate(
+                    [
+                        flat(ref[x + spread * ax, spread * ay : spread * ay + LENGTH])
+                        for ay in range(3)
+                    ],
+                    axis=1,
+                )
+                for x in range(ROWS)
+            ],
+            axis=0,
+        )
+        part[k] = matmul(slopes, cells).reshape(part.shape[1:])
 
     def coarse_window(x):
         return [flat(e3[x, r, j : j + HALF]) for r, j in ((0, 0), (1, 0), (0, 1))]
@@ -409,11 +461,14 @@
             total += matmul(gt[qx], cells)
         part[k] = total.reshape(part.shape[1:])
 
-    for k in range(3):
-        grads(k, e2, 2)
-        advance(*range(k + 1))
+    grads(0, e2, 2)
+    advance(0)
+    grads(1, e2, 2)
+    advance(1, 0)
+    grads(2, e2, 2)
+    advance(2, 1, 0)
     arrived(halo_three)
-    get_v3f.wait()
+    ready(get_v3f)
 
     @pl.when(space == 0)
     def _():
@@ -425,19 +480,19 @@
 
     for k in range(3, 6):
         coarse_grads(k)
-        advance(*range(k + 1))
+        advance(k)
     for qx in range(2):
         cells = [block for ax in range(3) for block in coarse_window(2 * qx + ax)]
-        cf[...] = combined(matmul(jnp.concatenate(cells, axis=1), v3f[...]), 1, False)
+        cf[...] = combined(matmul_transposed(jnp.concatenate(cells, axis=1), taps_of(v3f)), 1, False)
         for qz in range(DEPTH // 2):
             coarse[qx, qz] = cf[pl.ds(2 * qz, HALF, stride=DEPTH), :].astype(BF)
-    advance(*range(6))
-    get_v2b.wait()
+    advance(0, 1, 2)
+    ready(get_v2b)
     arrived(halo_four)
     clear(e4, 2)
 
     def layer_back(x, half):
-        back = combined(matmul(mirror(x, half), v2b[...]), 2, True).astype(BF).astype(F32)
+        back = combined(matmul(mirror(x, half), v2b[...].reshape(TAPS, WIDE)), 2, True).astype(BF).astype(F32)
         slope = (back * d1[x, half]).astype(BF)
         store_transposed(st, 2 * x + half, slope.astype(F32), 1)
 
@@ -451,38 +506,43 @@
             axis=1,
         )
 
-    over(0, 4, layer_back)
-    advance(*range(6))
-    over(4, 8, layer_back)
-    advance(*range(6))
-    for k in range(6, 9):
-        grads(k, e1, 1)
-        advance(*range(k + 1))
+    over(0, 2, layer_back)
+    advance(2, 3, 4, 5)
+    over(2, 4, layer_back)
+    advance(0, 1)
+    over(4, 6, layer_back)
+    advance(2, 3, 4, 5)
+    over(6, 8, layer_back)
+    advance(0, 1, 2)
+    grads(6, e1, 1)
+    advance(6, 3, 4, 5)
+    grads(7, e1, 1)
+    advance(7, 6, 1, 2)
+    grads(8, e1, 1)
+    advance(8, 7, 6, 3, 4, 5)
     while any(progress[k] < len(stages) for k in range(CHUNKS)):
-        advance(*range(CHUNKS))
+        advance(*range(CHUNKS - 4, CHUNKS), *range(CHUNKS - 4))
     for copy in started:
         copy.wait_send()
 
 
 def local(features, fluid_tiles, weight_one, weight_two, weight_three, upstream, sizes):
     n_space, n_chan = sizes
-    feat = jnp.transpose(features, (0, 2, 1, 3))
-    up = jnp.transpose(upstream, (0, 2, 1, 3))
-    up = jnp.stack([up, jnp.zeros_like(up)], axis=3).reshape(2, HALF, DEPTH, CH)
-    tiles = jnp.transpose(fluid_tiles[0], (1, 0)).astype(F32)
-    mask = jnp.broadcast_to(jnp.repeat(tiles, TILE_Z, axis=1)[:, :, None], (2, DEPTH, CH))
-
-    def forward(weight):
-        return jnp.transpose(weight, (1, 3, 4, 2, 0)).reshape(TAPS, WIDE)
-
-    def backward(weight):
-        return jnp.transpose(weight, (1, 3, 0, 2, 4)).reshape(TAPS, WIDE)
+    tiles = jnp.transpose(fluid_tiles, (0, 2, 1))
+
+    def by_tap(weight):
+        return jnp.transpose(weight, (1, 2, 3, 0, 4))
+
+    def by_output(grad):
+        return jnp.transpose(grad.reshape(3, 3, 3, 2 * 16, CH), (3, 0, 1, 2, 4))
 
     hbm = pl.BlockSpec(memory_space=pl.ANY)
     vmem = pl.BlockSpec(memory_space=pltpu.VMEM)
-    grad_shape = jax.ShapeDtypeStruct((2, 16, 3 * TAPS), F32)
+    smem = pl.BlockSpec(memory_space=pltpu.SMEM)
+    grad_shape = jax.ShapeDtypeStruct((3, 3, 3, 2, 16, CH), F32)
     copies = 31 + 11 * CHUNKS
-    weight_shape = pltpu.VMEM((TAPS, WIDE), BF)
+    forward_shape = pltpu.VMEM((3, 3, 3, CH, CH), BF)
+    backward_shape = pltpu.VMEM((3, 3, CH, WIDE), BF)
     piece = (CHUNKS, 3, 16, WIDE)
     pieces = (CHUNKS, 3, 3, 16, WIDE)
     coarse, grad_one, grad_two, grad_three = pl.pallas_call(
@@ -493,7 +553,7 @@
             grad_shape,
             grad_shape,
         ),
-        in_specs=[hbm, hbm, vmem, hbm, hbm, hbm, hbm, hbm],
+        in_specs=[hbm, hbm, smem, hbm, hbm, hbm],
         out_specs=[vmem] * 4,
         scratch_shapes=[
             pltpu.VMEM((ROWS + 2, LENGTH + 2, DEPTH, CH), BF),
@@ -503,14 +563,17 @@
             pltpu.VMEM((3, HALF + 1, DEPTH, CH), BF),
             pltpu.VMEM((ROWS, 2, CELLS, CH), F32),
             pltpu.VMEM((ROWS, 2, HALF, DEPTH, CH), BF),
-            weight_shape,
-            weight_shape,
-            weight_shape,
-            weight_shape,
-            weight_shape,
+            forward_shape,
+            forward_shape,
+            forward_shape,
+            backward_shape,
+            backward_shape,
             pltpu.VMEM((8, WIDE, CELLS), BF),
             pltpu.VMEM((2, WIDE, CELLS), BF),
             pltpu.VMEM((CELLS, CH), F32),
+            pltpu.VMEM((ROWS, DEPTH, LENGTH, CH), BF),
+            pltpu.VMEM((2, DEPTH // 2, HALF, CH), BF),
+            pltpu.VMEM((LENGTH * DEPTH, CH), F32),
             pltpu.VMEM((CHUNKS, 3, n_chan, 2, 16, WIDE), F32),
             pltpu.VMEM((CHUNKS, 3, n_chan, 16, WIDE), BF),
             pltpu.VMEM((CHUNKS, 3, n_chan, 16, WIDE), BF),
@@ -520,32 +583,24 @@
             pltpu.VMEM(pieces, BF),
             pltpu.VMEM(piece, BF),
             pltpu.VMEM(pieces, BF),
-            pltpu.VMEM((CHUNKS, 16, TAPS), F32),
-            pltpu.VMEM((CHUNKS, 16, TAPS), F32),
+            pltpu.VMEM(piece, F32),
+            pltpu.VMEM(piece, F32),
             pltpu.SemaphoreType.DMA((copies,)),
             pltpu.SemaphoreType.DMA((copies,)),
-            pltpu.SemaphoreType.DMA((7,)),
+            pltpu.SemaphoreType.DMA((17,)),
         ],
         compiler_params=pltpu.CompilerParams(
             collective_id=0, has_side_effects=True, vmem_limit_bytes=58 << 20
         ),
     )(
-        feat,
-        up,
-        mask,
-        forward(weight_one),
-        forward(weight_two),
-        forward(weight_three),
-        backward(weight_two),
-        backward(weight_three),
+        features,
+        upstream,
+        tiles,
+        by_tap(weight_one),
+        by_tap(weight_two),
+        by_tap(weight_three),
     )
-    shape = (2 * 16, 3, 3, 3, CH)
-    return (
-        coarse,
-        grad_one.reshape(shape),
-        grad_two.reshape(shape),
-        grad_three.reshape(shape),
-    )
+    return coarse, by_output(grad_one), by_output(grad_two), by_output(grad_three)
 
 
 def solution(mesh):

time: 135 us -> 109 us (0.81)
  Pallas kernels: 116 us -> 102 us
  local copies, waits for them, and re-layouts: 18.4 us -> 5.36 us
    pallas_call x1, Pallas kernels: 116 us -> 102 us  [local(): pl.pallas_call(functools.partial(program, n_space, n_chan), out_shape=(ja...]
    transpose x5 -> x0, local copies, waits for them, and re-layouts: 5.31 us -> none  [the longest x2 2.78 us: backward(): return jnp.transpose(weight, (1, 3, 0, 2, 4)).reshape(TAPS, WIDE)]
    reshape x5 -> x0, local copies, waits for them, and re-layouts: 4.72 us -> none  [the longest x1 1.6 us: backward(): return jnp.transpose(weight, (1, 3, 0, 2, 4)).reshape(TAPS, WIDE)]
    unnamed x25 -> x8, local copies, waits for them, and re-layouts: 6.54 us -> 5.36 us
where the time goes in v1:
time: 109 us; the launch traced here: 108 us
  Pallas kernels  102 us (94%)
  local copies, waits for them, and re-layouts  5.36 us (5%)
    pallas_call x1, Pallas kernels, local(): pl.pallas_call(functools.partial(program, n_space, n_chan), out_shape=(ja...  102 us
    unnamed x8, local copies, waits for them, and re-layouts  5.36 us

profile of v1, /device:TPU:1, one launch (start us, length us, event | category | flops | bytes accessed | tf_op | source)
XLA Modules:
  0.0 108.4 jit_solution(10777586896415097971)
XLA Ops:
  0.6 102.4 %shard_map.93 = (bf16[2,8,32,128]{3,2,1,0:T(8,128)(2,1)}, f32[3,3,3,2,16,128]{5,4,3,2,1,0:T(8,128)}, f32[3,3,3,2,16,128]{5,4,3,2,1,0:T(8,128)}, f32[3,3,3,2,16,128]{5,4,3,2,1,0:T(8,128)}) custom-call(bf16[4,16,64,128]{3,2,1,0:T(8,128)(2,1)} %feat.1, bf16[2,8,32,128]{3,2,1,0:T(8,128)(2,1)} %up.1, s32[1,2,4]{2,1,0:T(2,128)} %bitcast.19, ...), custom_call_target="tpu_custom_call" | custom-call | tf_op jit(solution)/shard_map/pallas_call | solution.py:548
  103.0 1.6 %copy.14 = bf16[2,8,32,128]{3,2,1,0:T(8,128)(2,1)} copy(bf16[2,8,32,128]{3,2,1,0:T(8,128)(2,1)} %get-tuple-element.16) | data formatting | bytes 262144
  104.6 0.0 copy-start.1
  104.6 1.9 %copy.15 = f32[32,3,3,3,128]{4,0,3,2,1:T(8,128)} copy(f32[32,3,3,3,128]{4,0,3,2,1:T(8,128)} %bitcast.18) | data formatting | bytes 884736
  106.5 0.0 copy-done.1
  106.5 0.0 copy-start
  106.5 0.8 copy.16
  107.2 0.4 copy-done
  107.7 0.8 copy.17
Async XLA Ops:
  104.6 1.9 %copy-start.1 = (f32[3,3,3,2,16,128]{5,4,3,2,1,0:T(8,128)S(1)}, f32[3,3,3,2,16,128]{5,4,3,2,1,0:T(8,128)}, u32[]{:S(2)}) copy-start(f32[3,3,3,2,16,128]{5,4,3,2,1,0:T(8,128)} %get-tuple-element.10) | copy-start | bytes 1327108
  106.5 1.2 %copy-start = (f32[3,3,3,2,16,128]{5,4,3,2,1,0:T(8,128)S(1)}, f32[3,3,3,2,16,128]{5,4,3,2,1,0:T(8,128)}, u32[]{:S(2)}) copy-start(f32[3,3,3,2,16,128]{5,4,3,2,1,0:T(8,128)} %get-tuple-element.11) | copy-start | bytes 1327108

commit v2 on v1

--- a/solution.py
+++ b/solution.py
@@ -208,16 +208,21 @@
 
     in_x, in_y = pl.ds(1, ROWS), pl.ds(1, LENGTH)
     top, right = ROWS, LENGTH
-    halo_one = [
-        send(e1.at[top, in_y], e1.at[0, in_y], near(1, 0)),
-        send(e1.at[1, in_y], e1.at[top + 1, in_y], near(-1, 0)),
+    sides = [
         send(e1.at[in_x, right], e1.at[in_x, 0], near(0, 1)),
         send(e1.at[in_x, 1], e1.at[in_x, right + 1], near(0, -1)),
+    ]
+    below = [
         send(e1.at[top, right], e1.at[0, 0], near(1, 1)),
         send(e1.at[top, 1], e1.at[0, right + 1], near(1, -1)),
+        send(e1.at[top, in_y], e1.at[0, in_y], near(1, 0)),
+    ]
+    above = [
         send(e1.at[1, right], e1.at[top + 1, 0], near(-1, 1)),
         send(e1.at[1, 1], e1.at[top + 1, right + 1], near(-1, -1)),
+        send(e1.at[1, in_y], e1.at[top + 1, in_y], near(-1, 0)),
     ]
+    due_one = {0: below, 1: sides, 2: [], 3: [], 4: [], top + 1: above}
     halo_up = [
         send(eu.at[0, pl.ds(0, HALF)], eu.at[2, pl.ds(0, HALF)], near(-1, 0)),
         send(eu.at[pl.ds(0, 2), 0], eu.at[pl.ds(0, 2), HALF], near(0, -1)),
@@ -228,44 +233,49 @@
         for copy in copies:
             copy.wait_recv()
 
-    def clear(ref, width):
+    def clear(ref, row, width):
         rows, columns = ref.shape[0], ref.shape[1]
-
-        @pl.when(space == 0)
-        def _():
-            ref[0:width] = jnp.zeros((width, columns, DEPTH, CH), BF)
-
-        @pl.when(space == n_space - 1)
-        def _():
-            ref[rows - width : rows] = jnp.zeros((width, columns, DEPTH, CH), BF)
+        line = jnp.zeros((columns, DEPTH, CH), BF)
+        corner = jnp.zeros((width, DEPTH, CH), BF)
+        if row < width:
+
+            @pl.when(space == 0)
+            def _():
+                ref[row] = line
+
+        if row >= rows - width:
+
+            @pl.when(space == n_space - 1)
+            def _():
+                ref[row] = line
 
         @pl.when(chan == 0)
         def _():
-            ref[:, 0:width] = jnp.zeros((rows, width, DEPTH, CH), BF)
+            ref[row, 0:width] = corner
 
         @pl.when(chan == n_chan - 1)
         def _():
-            ref[:, columns - width : columns] = jnp.zeros((rows, width, DEPTH, CH), BF)
-
-    def rim(ref, low):
-        y = pl.ds(2, LENGTH)
-        if low:
-            near_rows, far_rows, to = pl.ds(2, 2), pl.ds(ROWS + 2, 2), -1
-        else:
-            near_rows, far_rows, to = pl.ds(ROWS, 2), pl.ds(0, 2), 1
-        first, last = pl.ds(2, 2), pl.ds(LENGTH, 2)
+            ref[row, columns - width : columns] = corner
+
+    def need(ref, due, width, *rows):
+        for row in rows:
+            if row in due:
+                arrived(due.pop(row))
+                clear(ref, row, width)
+
+    def spread_row(ref, due, x):
+        own = x + 2
+        far, to = (own + ROWS, -1) if x < 2 else (own - ROWS, 1)
+        first, last, y = pl.ds(2, 2), pl.ds(LENGTH, 2), pl.ds(2, LENGTH)
         before, after = pl.ds(0, 2), pl.ds(LENGTH + 2, 2)
-        return [
-            send(ref.at[near_rows, y], ref.at[far_rows, y], near(to, 0)),
-            send(ref.at[near_rows, last], ref.at[far_rows, before], near(to, 1)),
-            send(ref.at[near_rows, first], ref.at[far_rows, after], near(to, -1)),
+        due[own] = [
+            send(ref.at[own, last], ref.at[own, before], near(0, 1)),
+            send(ref.at[own, first], ref.at[own, after], near(0, -1)),
         ]
-
-    def sides(ref):
-        x = pl.ds(2, ROWS)
-        return [
-            send(ref.at[x, pl.ds(LENGTH, 2)], ref.at[x, pl.ds(0, 2)], near(0, 1)),
-            send(ref.at[x, pl.ds(2, 2)], ref.at[x, pl.ds(LENGTH + 2, 2)], near(0, -1)),
+        due[far] = [
+            send(ref.at[own, last], ref.at[far, before], near(to, 1)),
+            send(ref.at[own, first], ref.at[far, after], near(to, -1)),
+            send(ref.at[own, y], ref.at[far, y], near(to, 0)),
         ]
 
     def flat(block):
@@ -304,8 +314,6 @@
         store_transposed(gt, qx, flat(eu[qx, 0:HALF]).astype(F32), 1)
 
     ready(get_v1f)
-    arrived(halo_one)
-    clear(e1, 1)
 
     def layer_one(x, half):
         pre = combined(matmul_transposed(window(e1, x, half * HALF, 1), taps_of(v1f)), 1, False)
@@ -315,11 +323,17 @@
         e2[2 + x, pl.ds(2 + half * HALF, HALF)] = block
         d1[x, half] = slope * inside
 
-    over(0, 4, layer_one)
-    halo_two = rim(e2, True)
-    over(4, 8, layer_one)
-    halo_two += rim(e2, False)
-    halo_two += sides(e2)
+    due_two, due_four = {}, {}
+    need(e1, due_one, 1, 1, 2, 3, 4)
+    over(2, 6, layer_one)
+    spread_row(e2, due_two, 1)
+    spread_row(e2, due_two, 2)
+    need(e1, due_one, 1, 0)
+    over(0, 2, layer_one)
+    spread_row(e2, due_two, 0)
+    need(e1, due_one, 1, top + 1)
+    over(6, 8, layer_one)
+    spread_row(e2, due_two, 3)
 
     arrived(halo_up)
     ready(get_v3b)
@@ -345,8 +359,6 @@
                 b2[2 * qx + px, py] = back.astype(BF).reshape(HALF, DEPTH, CH)
 
     ready(get_v2f)
-    arrived(halo_two)
-    clear(e2, 2)
 
     def layer_two(x, half):
         pre = combined(matmul_transposed(window(e2, x, half * HALF, 2), taps_of(v2f)), 2, False)
@@ -362,65 +374,85 @@
         e4[2 + x, pl.ds(2 + half * HALF, HALF)] = product.reshape(HALF, DEPTH, CH)
         store_transposed(st, 2 * x + half, product.astype(F32), 2)
 
-    over(0, 4, layer_two)
-    halo_four = rim(e4, True)
-    over(4, 8, layer_two)
-    halo_four += rim(e4, False)
-    halo_four += sides(e4)
     evens, odds = pl.ds(0, HALF), pl.ds(1, HALF)
-    halo_three = [
-        send(e3.at[ROWS, 1, evens], e3.at[0, 1, evens], near(1, 0)),
-        send(e3.at[ROWS, 0, odds], e3.at[0, 0, odds], near(1, 0)),
-        send(e3.at[pl.ds(1, ROWS), 0, HALF], e3.at[pl.ds(1, ROWS), 0, 0], near(0, 1)),
-        send(e3.at[ROWS, 0, HALF], e3.at[0, 0, 0], near(1, 1)),
-    ]
+    inner = pl.ds(1, ROWS)
+    halo_three = []
+    for x in (3, 2, 1, 0):
+        need(e2, due_two, 2, x, x + 2, x + 4)
+        over(2 * x, 2 * x + 2, layer_two)
+        spread_row(e4, due_four, x)
+        if x == 3:
+            halo_three += [
+                send(e3.at[ROWS, 0, HALF], e3.at[0, 0, 0], near(1, 1)),
+                send(e3.at[ROWS, 1, evens], e3.at[0, 1, evens], near(1, 0)),
+                send(e3.at[ROWS, 0, odds], e3.at[0, 0, odds], near(1, 0)),
+            ]
+    halo_three.append(send(e3.at[inner, 0, HALF], e3.at[inner, 0, 0], near(0, 1)))
 
     waits = {}
 
+    def place(k):
+        if k < CHUNKS - 1:
+            return k, slice(None)
+        j = k - (CHUNKS - 1)
+        return CHUNKS - 1, slice(j * CH, (j + 1) * CH)
+
     def share_core(k):
-        cs[k] = part[k, :, :, 1 - core].astype(BF)
-        waits[k] = [send(cs.at[k], cr.at[k], sibling)]
+        b, w = place(k)
+        cs[b, :, :, :, w] = part[b, :, :, 1 - core, :, w].astype(BF)
+        waits[k] = [send(cs.at[b, :, :, :, w], cr.at[b, :, :, :, w], sibling)]
 
     def share_chan(k):
+        b, w = place(k)
         arrived(waits[k])
         waits[k] = []
+        for d in (2, 1, 3)[: n_chan - 1]:
+            other = lax.rem(chan + d, n_chan)
+            total = part[b, :, other, core, :, w] + cr[b, :, other, :, w].astype(F32)
+            zs[b, d - 1, :, :, w] = total.astype(BF)
+            block = (b, d - 1, slice(None), slice(None), w)
+            waits[k].append(send(zs.at[block], zr.at[block], near(0, d)))
+
+    def scatter(k, source, target, peer):
+        b, w = place(k)
+        waits[k] = [
+            send(source.at[b, :, :, w], target.at[b, d - 1, :, :, w], peer(d)) for d in (2, 1, 3)
+        ]
+
+    def share_first(k):
+        b, w = place(k)
+        arrived(waits[k])
+        total = part[b, :, chan, core, :, w] + cr[b, :, chan, :, w].astype(F32)
         for d in range(1, n_chan):
-            other = lax.rem(chan + d, n_chan)
-            zs[k, d - 1] = (part[k, :, other, core] + cr[k, :, other].astype(F32)).astype(BF)
-            waits[k].append(send(zs.at[k, d - 1], zr.at[k, d - 1], near(0, d)))
-
-    def share_first(k):
+            total += zr[b, d - 1, :, :, w].astype(F32)
+        xs[b, :, :, w] = total.astype(BF)
+        scatter(k, xs, xr, (x_peer, y_peer)[k % 2])
+
+    def four(own, others, k):
+        b, w = place(k)
+        opposite = own[b, :, :, w].astype(F32) + others[b, 1, :, :, w].astype(F32)
+        return opposite + (others[b, 0, :, :, w].astype(F32) + others[b, 2, :, :, w].astype(F32))
+
+    def share_second(k):
+        b, w = place(k)
         arrived(waits[k])
-        total = part[k, :, chan, core] + cr[k, :, chan].astype(F32)
-        for d in range(1, n_chan):
-            total += zr[k, d - 1].astype(F32)
-        xs[k] = total.astype(BF)
-        peer = (x_peer, y_peer)[k % 2]
-        waits[k] = [send(xs.at[k], xr.at[k, d - 1], peer(d)) for d in range(1, CHIPS)]
-
-    def four(own, others, k):
-        opposite = own[k].astype(F32) + others[k, 1].astype(F32)
-        return opposite + (others[k, 0].astype(F32) + others[k, 2].astype(F32))
-
-    def share_second(k):
+        ys[b, :, :, w] = four(xs, xr, k).astype(BF)
+        scatter(k, ys, yr, (y_peer, x_peer)[k % 2])
+
+    def share_back(k):
+        b, w = place(k)
         arrived(waits[k])
-        ys[k] = four(xs, xr, k).astype(BF)
-        peer = (y_peer, x_peer)[k % 2]
-        waits[k] = [send(ys.at[k], yr.at[k, d - 1], peer(d)) for d in range(1, CHIPS)]
-
-    def share_back(k):
+        fs[b, :, :, w] = four(ys, yr, k)
+        waits[k] = [send(fs.at[b, :, :, w], fr.at[b, :, :, w], sibling)]
+
+    def finish(k):
+        b, _ = place(k)
         arrived(waits[k])
-        total = four(ys, yr, k)
-        fs[k] = total
-        waits[k] = [send(fs.at[k], fr.at[k], sibling)]
-
-    def finish(k):
-        arrived(waits[k])
-        out = (out2, out3, out1)[k // 3]
-        for ay in range(3):
+        out = (out2, out3, out1)[b // 3]
+        for ay in range(3) if b == k and k < CHUNKS - 1 else (k - CHUNKS + 1,):
             columns = slice(ay * CH, (ay + 1) * CH)
-            out[k % 3, :, ay, core] = fs[k, :, :, columns]
-            out[k % 3, :, ay, 1 - core] = fr[k, :, :, columns]
+            out[b % 3, :, ay, core] = fs[b, :, :, columns]
+            out[b % 3, :, ay, 1 - core] = fr[b, :, :, columns]
 
     stages = (share_core, share_chan, share_first, share_second, share_back, finish)
     progress = {}
@@ -464,9 +496,9 @@
     grads(0, e2, 2)
     advance(0)
     grads(1, e2, 2)
-    advance(1, 0)
+    advance(1)
     grads(2, e2, 2)
-    advance(2, 1, 0)
+    advance(2, 0)
     arrived(halo_three)
     ready(get_v3f)
 
@@ -481,15 +513,16 @@
     for k in range(3, 6):
         coarse_grads(k)
         advance(k)
-    for qx in range(2):
+
+    def coarse_rows(qx):
         cells = [block for ax in range(3) for block in coarse_window(2 * qx + ax)]
-        cf[...] = combined(matmul_transposed(jnp.concatenate(cells, axis=1), taps_of(v3f)), 1, False)
+        cells = jnp.concatenate(cells, axis=1)
+        cf[...] = combined(matmul_transposed(cells, taps_of(v3f)), 1, False)
         for qz in range(DEPTH // 2):
             coarse[qx, qz] = cf[pl.ds(2 * qz, HALF, stride=DEPTH), :].astype(BF)
-    advance(0, 1, 2)
+
+    advance(1)
     ready(get_v2b)
-    arrived(halo_four)
-    clear(e4, 2)
 
     def layer_back(x, half):
         back = combined(matmul(mirror(x, half), v2b[...].reshape(TAPS, WIDE)), 2, True).astype(BF).astype(F32)
@@ -506,24 +539,38 @@
             axis=1,
         )
 
-    over(0, 2, layer_back)
-    advance(2, 3, 4, 5)
-    over(2, 4, layer_back)
-    advance(0, 1)
-    over(4, 6, layer_back)
-    advance(2, 3, 4, 5)
-    over(6, 8, layer_back)
-    advance(0, 1, 2)
+    for x in (1, 0, 3, 2):
+        need(e4, due_four, 2, x, x + 2, x + 4)
+        over(2 * x, 2 * x + 2, layer_back)
+        advance(*((2, 0) if x in (1, 3) else (3, 4, 5, 1)))
     grads(6, e1, 1)
-    advance(6, 3, 4, 5)
+    advance(6, 2, 0)
     grads(7, e1, 1)
-    advance(7, 6, 1, 2)
+    advance(7, 3, 4, 5)
     grads(8, e1, 1)
-    advance(8, 7, 6, 3, 4, 5)
-    while any(progress[k] < len(stages) for k in range(CHUNKS)):
-        advance(*range(CHUNKS - 4, CHUNKS), *range(CHUNKS - 4))
+    advance(8, 9, 10, 6, 1)
+    coarse_rows(0)
+    advance(7, 0, 2)
+    coarse_rows(1)
+    advance(8, 9, 10, 3, 4, 5, 6, 1, 7, 2)
+    last = (6, 7, 8, 9, 10)
+    advance(8, 9, 10, 6, 3, 4, 5, 7)
+    while any(progress[k] < len(stages) for k in last):
+        advance(*last)
     for copy in started:
         copy.wait_send()
+
+
+def write_out(*refs):
+    count = len(refs) // 2
+    sources, targets, sems = refs[:count], refs[count:-1], refs[-1]
+    copies = [
+        pltpu.make_async_copy(a, b, sems.at[i]) for i, (a, b) in enumerate(zip(sources, targets))
+    ]
+    for copy in copies:
+        copy.start()
+    for copy in copies:
+        copy.wait()
 
 
 def local(features, fluid_tiles, weight_one, weight_two, weight_three, upstream, sizes):
@@ -540,12 +587,12 @@
     vmem = pl.BlockSpec(memory_space=pltpu.VMEM)
     smem = pl.BlockSpec(memory_space=pltpu.SMEM)
     grad_shape = jax.ShapeDtypeStruct((3, 3, 3, 2, 16, CH), F32)
-    copies = 31 + 11 * CHUNKS
+    copies = 55 + 11 * (CHUNKS + 2)
     forward_shape = pltpu.VMEM((3, 3, 3, CH, CH), BF)
     backward_shape = pltpu.VMEM((3, 3, CH, WIDE), BF)
     piece = (CHUNKS, 3, 16, WIDE)
     pieces = (CHUNKS, 3, 3, 16, WIDE)
-    coarse, grad_one, grad_two, grad_three = pl.pallas_call(
+    results = pl.pallas_call(
         functools.partial(program, n_space, n_chan),
         out_shape=(
             jax.ShapeDtypeStruct((2, DEPTH // 2, HALF, CH), BF),
@@ -600,6 +647,13 @@
         by_tap(weight_two),
         by_tap(weight_three),
     )
+    coarse, grad_one, grad_two, grad_three = pl.pallas_call(
+        write_out,
+        out_shape=tuple(jax.ShapeDtypeStruct(r.shape, r.dtype) for r in results),
+        in_specs=[hbm] * 4,
+        out_specs=[hbm] * 4,
+        scratch_shapes=[pltpu.SemaphoreType.DMA((4,))],
+    )(*results)
     return coarse, by_output(grad_one), by_output(grad_two), by_output(grad_three)
 
 

time: 109 us -> 128 us (1.17)
  Pallas kernels: 102 us -> 127 us
  local copies, waits for them, and re-layouts: 5.36 us -> 0 us
    pallas_call x0 -> x1, Pallas kernels: none -> 45.3 us  [local(): pl.pallas_call(write_out, out_shape=tuple((jax.ShapeDtypeStruct(r.shape,...]
    pallas_call x1, Pallas kernels: 102 us -> 81.5 us  [local(): pl.pallas_call(functools.partial(program, n_space, n_chan), out_shape=(ja...]
    unnamed x8 -> x0, local copies, waits for them, and re-layouts: 5.36 us -> none
where the time goes in v2:
time: 128 us
  Pallas kernels  127 us (99%)
    pallas_call x1, Pallas kernels, local(): pl.pallas_call(functools.partial(program, n_space, n_chan), out_shape=(ja...  81.5 us
    pallas_call x1, Pallas kernels, local(): pl.pallas_call(write_out, out_shape=tuple((jax.ShapeDtypeStruct(r.shape,...  45.3 us

profile of v2, /device:TPU:1, one launch (start us, length us, event | category | flops | bytes accessed | tf_op | source)
XLA Modules:
  0.0 127.6 jit_solution(120923027320860135)
XLA Ops:
  0.6 81.5 %shard_map.93 = (bf16[2,8,32,128]{3,2,1,0:T(8,128)(2,1)}, f32[3,3,3,2,16,128]{5,4,3,2,1,0:T(8,128)}, f32[3,3,3,2,16,128]{5,4,3,2,1,0:T(8,128)}, f32[3,3,3,2,16,128]{5,4,3,2,1,0:T(8,128)}) custom-call(bf16[4,16,64,128]{3,2,1,0:T(8,128)(2,1)} %feat.1, bf16[2,8,32,128]{3,2,1,0:T(8,128)(2,1)} %up.1, s32[1,2,4]{2,1,0:T(2,128)} %bitcast.16, ...), custom_call_target="tpu_custom_call" | custom-call | tf_op jit(solution)/shard_map/pallas_call | solution.py:595
  82.1 45.3 %shard_map.94 = (bf16[2,8,32,128]{3,2,1,0:T(8,128)(2,1)}, f32[3,3,3,2,16,128]{5,4,3,2,1,0:T(8,128)}, f32[3,3,3,2,16,128]{5,4,3,2,1,0:T(8,128)}, f32[3,3,3,2,16,128]{5,4,3,2,1,0:T(8,128)}) custom-call(bf16[2,8,32,128]{3,2,1,0:T(8,128)(2,1)} %get-tuple-element.12.refs_0_, f32[3,3,3,2,16,128]{5,4,3,2,1,0:T(8,128)} %get-tuple-element.13.refs_1_, ...), custom_call_target="tpu_custom_call" | custom-call | tf_op jit(solution)/shard_map/pallas_call | solution.py:650

commit v3 on v2

--- a/solution.py
+++ b/solution.py
@@ -562,14 +562,19 @@
 
 
 def write_out(*refs):
-    count = len(refs) // 2
-    sources, targets, sems = refs[:count], refs[count:-1], refs[-1]
-    copies = [
-        pltpu.make_async_copy(a, b, sems.at[i]) for i, (a, b) in enumerate(zip(sources, targets))
+    sources, targets, staged, sems = refs[:4], refs[4:8], refs[8:12], refs[12]
+    loads = [
+        pltpu.make_async_copy(a, b, sems.at[i]) for i, (a, b) in enumerate(zip(sources, staged))
     ]
-    for copy in copies:
+    stores = [
+        pltpu.make_async_copy(a, b, sems.at[4 + i]) for i, (a, b) in enumerate(zip(staged, targets))
+    ]
+    for copy in loads:
         copy.start()
-    for copy in copies:
+    for load, store in zip(loads, stores):
+        load.wait()
+        store.start()
+    for copy in stores:
         copy.wait()
 
 
@@ -652,7 +657,8 @@
         out_shape=tuple(jax.ShapeDtypeStruct(r.shape, r.dtype) for r in results),
         in_specs=[hbm] * 4,
         out_specs=[hbm] * 4,
-        scratch_shapes=[pltpu.SemaphoreType.DMA((4,))],
+        scratch_shapes=[pltpu.VMEM(r.shape, r.dtype) for r in results]
+        + [pltpu.SemaphoreType.DMA((8,))],
     )(*results)
     return coarse, by_output(grad_one), by_output(grad_two), by_output(grad_three)
 

time: 128 us -> 84.6 us (0.66)
  Pallas kernels: 127 us -> 83.7 us
    pallas_call x1, Pallas kernels: 45.3 us -> 2.21 us  [local(): pl.pallas_call(write_out, out_shape=tuple((jax.ShapeDtypeStruct(r.shape,...]
where the time goes in v3:
time: 84.6 us; the launch traced here: 84.5 us
  Pallas kernels  83.7 us (99%)
    pallas_call x1, Pallas kernels, local(): pl.pallas_call(functools.partial(program, n_space, n_chan), out_shape=(ja...  81.5 us
    pallas_call x1, Pallas kernels, local(): pl.pallas_call(write_out, out_shape=tuple((jax.ShapeDtypeStruct(r.shape,...  2.21 us

profile of v3, /device:TPU:1, one launch (start us, length us, event | category | flops | bytes accessed | tf_op | source)
XLA Modules:
  0.0 84.5 jit_solution(3658493944130911942)
XLA Ops:
  0.6 81.5 %shard_map.93 = (bf16[2,8,32,128]{3,2,1,0:T(8,128)(2,1)}, f32[3,3,3,2,16,128]{5,4,3,2,1,0:T(8,128)}, f32[3,3,3,2,16,128]{5,4,3,2,1,0:T(8,128)}, f32[3,3,3,2,16,128]{5,4,3,2,1,0:T(8,128)}) custom-call(bf16[4,16,64,128]{3,2,1,0:T(8,128)(2,1)} %feat.1, bf16[2,8,32,128]{3,2,1,0:T(8,128)(2,1)} %up.1, s32[1,2,4]{2,1,0:T(2,128)} %bitcast.16, ...), custom_call_target="tpu_custom_call" | custom-call | tf_op jit(solution)/shard_map/pallas_call | solution.py:600
  82.1 2.2 %shard_map.94 = (bf16[2,8,32,128]{3,2,1,0:T(8,128)(2,1)}, f32[3,3,3,2,16,128]{5,4,3,2,1,0:T(8,128)}, f32[3,3,3,2,16,128]{5,4,3,2,1,0:T(8,128)}, f32[3,3,3,2,16,128]{5,4,3,2,1,0:T(8,128)}) custom-call(bf16[2,8,32,128]{3,2,1,0:T(8,128)(2,1)} %get-tuple-element.12.refs_0_, f32[3,3,3,2,16,128]{5,4,3,2,1,0:T(8,128)} %get-tuple-element.13.refs_1_, ...), custom_call_target="tpu_custom_call" | custom-call | tf_op jit(solution)/shard_map/pallas_call | solution.py:655

commit v4 on v3

--- a/solution.py
+++ b/solution.py
@@ -454,6 +454,14 @@
             out[b % 3, :, ay, core] = fs[b, :, :, columns]
             out[b % 3, :, ay, 1 - core] = fr[b, :, :, columns]
 
+    left = []
+
+    def sent(keep):
+        while len(left) < len(started) - keep:
+            copy = started[len(left)]
+            copy.wait_send()
+            left.append(copy)
+
     stages = (share_core, share_chan, share_first, share_second, share_back, finish)
     progress = {}
 
@@ -550,15 +558,20 @@
     grads(8, e1, 1)
     advance(8, 9, 10, 6, 1)
     coarse_rows(0)
-    advance(7, 0, 2)
+    advance(8, 9, 10, 7, 0, 2)
     coarse_rows(1)
-    advance(8, 9, 10, 3, 4, 5, 6, 1, 7, 2)
-    last = (6, 7, 8, 9, 10)
-    advance(8, 9, 10, 6, 3, 4, 5, 7)
-    while any(progress[k] < len(stages) for k in last):
-        advance(*last)
-    for copy in started:
-        copy.wait_send()
+    sent(60)
+    advance(8, 9, 10, 6, 7)
+    advance(3, 4, 5, 1, 2)
+    sent(40)
+    advance(8, 9, 10, 6, 7)
+    advance(3, 4, 5)
+    sent(24)
+    advance(8, 9, 10, 6, 7)
+    sent(12)
+    advance(6, 7, 8, 9, 10)
+    sent(0)
+    assert all(progress[k] == len(stages) for k in range(CHUNKS + 2))
 
 
 def write_out(*refs):

time: 84.6 us -> 82.2 us (0.972)
  Pallas kernels: 83.7 us -> 81.2 us
    pallas_call x1, Pallas kernels: 81.5 us -> 79 us  [local(): pl.pallas_call(functools.partial(program, n_space, n_chan), out_shape=(ja...]
where the time goes in v4:
time: 82.2 us; the launch traced here: 82 us
  Pallas kernels  81.2 us (99%)
    pallas_call x1, Pallas kernels, local(): pl.pallas_call(functools.partial(program, n_space, n_chan), out_shape=(ja...  79 us
    pallas_call x1, Pallas kernels, local(): pl.pallas_call(write_out, out_shape=tuple((jax.ShapeDtypeStruct(r.shape,...  2.21 us

profile of v4, /device:TPU:1, one launch (start us, length us, event | category | flops | bytes accessed | tf_op | source)
XLA Modules:
  0.0 82.0 jit_solution(4185198307839587451)
XLA Ops:
  0.6 79.0 %shard_map.93 = (bf16[2,8,32,128]{3,2,1,0:T(8,128)(2,1)}, f32[3,3,3,2,16,128]{5,4,3,2,1,0:T(8,128)}, f32[3,3,3,2,16,128]{5,4,3,2,1,0:T(8,128)}, f32[3,3,3,2,16,128]{5,4,3,2,1,0:T(8,128)}) custom-call(bf16[4,16,64,128]{3,2,1,0:T(8,128)(2,1)} %feat.1, bf16[2,8,32,128]{3,2,1,0:T(8,128)(2,1)} %up.1, s32[1,2,4]{2,1,0:T(2,128)} %bitcast.16, ...), custom_call_target="tpu_custom_call" | custom-call | tf_op jit(solution)/shard_map/pallas_call | solution.py:613
  79.6 2.2 %shard_map.94 = (bf16[2,8,32,128]{3,2,1,0:T(8,128)(2,1)}, f32[3,3,3,2,16,128]{5,4,3,2,1,0:T(8,128)}, f32[3,3,3,2,16,128]{5,4,3,2,1,0:T(8,128)}, f32[3,3,3,2,16,128]{5,4,3,2,1,0:T(8,128)}) custom-call(bf16[2,8,32,128]{3,2,1,0:T(8,128)(2,1)} %get-tuple-element.12.refs_0_, f32[3,3,3,2,16,128]{5,4,3,2,1,0:T(8,128)} %get-tuple-element.13.refs_1_, ...), custom_call_target="tpu_custom_call" | custom-call | tf_op jit(solution)/shard_map/pallas_call | solution.py:668

commit v5 on v4

--- a/solution.py
+++ b/solution.py
@@ -392,10 +392,7 @@
     waits = {}
 
     def place(k):
-        if k < CHUNKS - 1:
-            return k, slice(None)
-        j = k - (CHUNKS - 1)
-        return CHUNKS - 1, slice(j * CH, (j + 1) * CH)
+        return k, slice(None)
 
     def share_core(k):
         b, w = place(k)
@@ -449,7 +446,7 @@
         b, _ = place(k)
         arrived(waits[k])
         out = (out2, out3, out1)[b // 3]
-        for ay in range(3) if b == k and k < CHUNKS - 1 else (k - CHUNKS + 1,):
+        for ay in range(3):
             columns = slice(ay * CH, (ay + 1) * CH)
             out[b % 3, :, ay, core] = fs[b, :, :, columns]
             out[b % 3, :, ay, 1 - core] = fr[b, :, :, columns]
@@ -556,22 +553,22 @@
     grads(7, e1, 1)
     advance(7, 3, 4, 5)
     grads(8, e1, 1)
-    advance(8, 9, 10, 6, 1)
+    advance(8, 6, 1)
     coarse_rows(0)
-    advance(8, 9, 10, 7, 0, 2)
+    advance(8, 7, 0, 2)
     coarse_rows(1)
     sent(60)
-    advance(8, 9, 10, 6, 7)
+    advance(8, 6, 7)
     advance(3, 4, 5, 1, 2)
     sent(40)
-    advance(8, 9, 10, 6, 7)
+    advance(8, 6, 7)
     advance(3, 4, 5)
     sent(24)
-    advance(8, 9, 10, 6, 7)
+    advance(8, 6, 7)
     sent(12)
-    advance(6, 7, 8, 9, 10)
+    advance(6, 7, 8)
     sent(0)
-    assert all(progress[k] == len(stages) for k in range(CHUNKS + 2))
+    assert all(progress[k] == len(stages) for k in range(CHUNKS))
 
 
 def write_out(*refs):
@@ -605,7 +602,7 @@
     vmem = pl.BlockSpec(memory_space=pltpu.VMEM)
     smem = pl.BlockSpec(memory_space=pltpu.SMEM)
     grad_shape = jax.ShapeDtypeStruct((3, 3, 3, 2, 16, CH), F32)
-    copies = 55 + 11 * (CHUNKS + 2)
+    copies = 55 + 11 * (CHUNKS)
     forward_shape = pltpu.VMEM((3, 3, 3, CH, CH), BF)
     backward_shape = pltpu.VMEM((3, 3, CH, WIDE), BF)
     piece = (CHUNKS, 3, 16, WIDE)

time: 82.2 us -> 81.7 us (level)
  no operation moved by 1% of the time
where the time goes in v5:
time: 81.7 us; the launch traced here: 81.5 us
  Pallas kernels  80.7 us (99%)
    pallas_call x1, Pallas kernels, local(): pl.pallas_call(functools.partial(program, n_space, n_chan), out_shape=(ja...  78.5 us
    pallas_call x1, Pallas kernels, local(): pl.pallas_call(write_out, out_shape=tuple((jax.ShapeDtypeStruct(r.shape,...  2.21 us

profile of v5, /device:TPU:1, one launch (start us, length us, event | category | flops | bytes accessed | tf_op | source)
XLA Modules:
  0.0 81.5 jit_solution(16323258973337138271)
XLA Ops:
  0.6 78.5 %shard_map.93 = (bf16[2,8,32,128]{3,2,1,0:T(8,128)(2,1)}, f32[3,3,3,2,16,128]{5,4,3,2,1,0:T(8,128)}, f32[3,3,3,2,16,128]{5,4,3,2,1,0:T(8,128)}, f32[3,3,3,2,16,128]{5,4,3,2,1,0:T(8,128)}) custom-call(bf16[4,16,64,128]{3,2,1,0:T(8,128)(2,1)} %feat.1, bf16[2,8,32,128]{3,2,1,0:T(8,128)(2,1)} %up.1, s32[1,2,4]{2,1,0:T(2,128)} %bitcast.16, ...), custom_call_target="tpu_custom_call" | custom-call | tf_op jit(solution)/shard_map/pallas_call | solution.py:610
  79.1 2.2 %shard_map.94 = (bf16[2,8,32,128]{3,2,1,0:T(8,128)(2,1)}, f32[3,3,3,2,16,128]{5,4,3,2,1,0:T(8,128)}, f32[3,3,3,2,16,128]{5,4,3,2,1,0:T(8,128)}, f32[3,3,3,2,16,128]{5,4,3,2,1,0:T(8,128)}) custom-call(bf16[2,8,32,128]{3,2,1,0:T(8,128)(2,1)} %get-tuple-element.12.refs_0_, f32[3,3,3,2,16,128]{5,4,3,2,1,0:T(8,128)} %get-tuple-element.13.refs_1_, ...), custom_call_target="tpu_custom_call" | custom-call | tf_op jit(solution)/shard_map/pallas_call | solution.py:665

commit v6 on v5

--- a/solution.py
+++ b/solution.py
@@ -555,7 +555,7 @@
     grads(8, e1, 1)
     advance(8, 6, 1)
     coarse_rows(0)
-    advance(8, 7, 0, 2)
+    advance(7, 0, 2, 8)
     coarse_rows(1)
     sent(60)
     advance(8, 6, 7)

time: 81.7 us -> 82.4 us (level)
  no operation moved by 1% of the time
where the time goes in v6:
time: 82.4 us; the launch traced here: 82.2 us
  Pallas kernels  81.4 us (99%)
    pallas_call x1, Pallas kernels, local(): pl.pallas_call(functools.partial(program, n_space, n_chan), out_shape=(ja...  79.2 us
    pallas_call x1, Pallas kernels, local(): pl.pallas_call(write_out, out_shape=tuple((jax.ShapeDtypeStruct(r.shape,...  2.21 us

profile of v6, /device:TPU:1, one launch (start us, length us, event | category | flops | bytes accessed | tf_op | source)
XLA Modules:
  0.0 82.2 jit_solution(4223251757256808721)
XLA Ops:
  0.6 79.2 %shard_map.93 = (bf16[2,8,32,128]{3,2,1,0:T(8,128)(2,1)}, f32[3,3,3,2,16,128]{5,4,3,2,1,0:T(8,128)}, f32[3,3,3,2,16,128]{5,4,3,2,1,0:T(8,128)}, f32[3,3,3,2,16,128]{5,4,3,2,1,0:T(8,128)}) custom-call(bf16[4,16,64,128]{3,2,1,0:T(8,128)(2,1)} %feat.1, bf16[2,8,32,128]{3,2,1,0:T(8,128)(2,1)} %up.1, s32[1,2,4]{2,1,0:T(2,128)} %bitcast.16, ...), custom_call_target="tpu_custom_call" | custom-call | tf_op jit(solution)/shard_map/pallas_call | solution.py:610
  79.9 2.2 %shard_map.94 = (bf16[2,8,32,128]{3,2,1,0:T(8,128)(2,1)}, f32[3,3,3,2,16,128]{5,4,3,2,1,0:T(8,128)}, f32[3,3,3,2,16,128]{5,4,3,2,1,0:T(8,128)}, f32[3,3,3,2,16,128]{5,4,3,2,1,0:T(8,128)}) custom-call(bf16[2,8,32,128]{3,2,1,0:T(8,128)(2,1)} %get-tuple-element.12.refs_0_, f32[3,3,3,2,16,128]{5,4,3,2,1,0:T(8,128)} %get-tuple-element.13.refs_1_, ...), custom_call_target="tpu_custom_call" | custom-call | tf_op jit(solution)/shard_map/pallas_call | solution.py:665
